TPU v7x, 32 devices: a whole 2x2x4 slice. The times are simulated.
32 devices in a mesh: groups: 2 (over y), ctx: 4 (over z), ch: 4 (over x, core).
Axes of the slice: x: 2, y: 2, z: 4, core: 2. Of those that a mesh axis runs over, the one named last changes fastest.
Arguments:
- projections: bfloat16 [1024, 3, 4096], P(('groups', 'ctx'), None, 'ch'), parts along dimension 0, may hold values from -6 to 6
- short_taps: float32 [3, 3, 4096], P(None, None, 'ch'), may hold values from -3 to 3
- residues: float32 [4096, 16], P(('ch', 'ctx')), may hold values from -2 to 2
- decay_rates: float32 [4096, 16], P(('ch', 'ctx')), may hold values from 0.25 to 16
- skip_gain: float32 [4096], P(('ch', 'ctx')), may hold values from -3 to 3
- grad_mixed: bfloat16 [1024, 2048], P(('groups', 'ctx'), 'ch'), parts along dimension 0, may hold values from -6 to 6
- out_weight: bfloat16 [4096, 2048], P('ch', 'ctx'), may hold values from -0.09375 to 0.09375
Outputs:
- grad_projections: bfloat16 [1024, 3, 4096], P(('groups', 'ctx'), None, 'ch'), parts along dimension 0
- grad_short: float32 [6, 3, 4096], P('groups', None, 'ch'), parts along dimension 0
- grad_skip: float32 [8192], P(('groups', 'ch', 'ctx')), parts along dimension 0
- grad_residues: float32 [8192, 16], P(('groups', 'ch', 'ctx')), parts along dimension 0
- grad_log_rates: float32 [8192, 16], P(('groups', 'ch', 'ctx')), parts along dimension 0
- grad_weight: float32 [8192, 2048], P(('groups', 'ch'), 'ctx'), parts along dimension 0
There are 2 independent parts, one for each index of `groups`. A program takes and returns all parts, laid end to end along the dimension named above; an argument that names none is the same for every part. Nothing has to cross between parts.
All inputs are finite; a program needn't handle non-finite values.
Results may differ from a plain program's by a relative error of at most 0.006.
Values may be sent and summed in bfloat16 or wider, within the bound.
A program may use at most 64 MiB of HBM per device.

v0:
```python
from functools import partial
import math
import jax
import jax.numpy as jnp
from jax import lax
from jax.sharding import PartitionSpec as P

SHORT = 3


def from_behind(x, axis, by):
    peers = lax.axis_size(axis)
    pairs = [(i, i + by) for i in range(peers) if 0 <= i + by < peers]
    return lax.ppermute(x, axis, pairs)


def make_filter(residues, decay_rates, seq_len):
    positions = jnp.arange(seq_len, dtype=jnp.float32) / seq_len
    amplitude = residues * jnp.sqrt(2.0 * decay_rates / seq_len)
    basis = jnp.exp(-decay_rates[:, :, None] * positions[None, None, :])
    return jnp.einsum("cn,cnt->ct", amplitude, basis, precision=lax.Precision.HIGHEST)


def circle(rows_count, cols_count, period):
    left_idx = jnp.arange(rows_count, dtype=jnp.int32)[:, None]
    right_idx = jnp.arange(cols_count, dtype=jnp.int32)[None, :]
    angle = (left_idx * right_idx % period).astype(jnp.float32) * (2.0 * math.pi / period)
    return (jnp.cos(angle), jnp.sin(angle))


def spectral_tables(length):
    factor_a = 1
    while factor_a * factor_a * 4 <= length and length % (factor_a * 2) == 0:
        factor_a = factor_a * 2
    factor_b = length // factor_a
    a_cos, a_sin = circle(factor_a, factor_a, factor_a)
    b_cos, b_sin = circle(factor_b, factor_b, factor_b)
    t_cos, t_sin = circle(factor_a, factor_b, length)
    return (length, factor_a, factor_b, a_cos, a_sin, b_cos, b_sin, t_cos, t_sin)


def forward_dft(signal, tables):
    length, factor_a, factor_b, a_cos, a_sin, b_cos, b_sin, t_cos, t_sin = tables
    highest = lax.Precision.HIGHEST
    channels, seq_len = signal.shape
    grid = jnp.pad(signal, ((0, 0), (0, length - seq_len))).reshape(channels, factor_a, factor_b)
    part_real = jnp.einsum("ka,cab->ckb", a_cos, grid, precision=highest)
    part_imag = -jnp.einsum("ka,cab->ckb", a_sin, grid, precision=highest)
    turn_real = part_real * t_cos + part_imag * t_sin
    turn_imag = part_imag * t_cos - part_real * t_sin
    out_real = jnp.einsum("ckb,bm->ckm", turn_real, b_cos, precision=highest) + jnp.einsum(
        "ckb,bm->ckm", turn_imag, b_sin, precision=highest
    )
    out_imag = jnp.einsum("ckb,bm->ckm", turn_imag, b_cos, precision=highest) - jnp.einsum(
        "ckb,bm->ckm", turn_real, b_sin, precision=highest
    )
    return (out_real, out_imag)


def inverse_dft(spec_real, spec_imag, seq_len, tables):
    length, factor_a, factor_b, a_cos, a_sin, b_cos, b_sin, t_cos, t_sin = tables
    highest = lax.Precision.HIGHEST
    channels = spec_real.shape[0]
    mid_real = jnp.einsum("ckm,mb->ckb", spec_real, b_cos, precision=highest) - jnp.einsum(
        "ckm,mb->ckb", spec_imag, b_sin, precision=highest
    )
    mid_imag = jnp.einsum("ckm,mb->ckb", spec_imag, b_cos, precision=highest) + jnp.einsum(
        "ckm,mb->ckb", spec_real, b_sin, precision=highest
    )
    turn_real = mid_real * t_cos - mid_imag * t_sin
    turn_imag = mid_imag * t_cos + mid_real * t_sin
    values = jnp.einsum("ak,ckb->cab", a_cos, turn_real, precision=highest) - jnp.einsum(
        "ak,ckb->cab", a_sin, turn_imag, precision=highest
    )
    return values.reshape(channels, length)[:, :seq_len] / length


def short_mix(extended, short_taps, tokens):
    running = jnp.zeros((tokens,) + extended.shape[1:], jnp.float32)
    for lag_index in range(SHORT):
        start_row = SHORT - 1 - lag_index
        running = running + short_taps[lag_index] * extended[start_row : start_row + tokens]
    return running


def mix_long(gate_cols, spec_h, gain, seq_len, tables):
    gate_f = gate_cols.astype(jnp.float32)
    u_real, u_imag = forward_dft(gate_f, tables)
    prod_real = spec_h[0] * u_real - spec_h[1] * u_imag
    prod_imag = spec_h[0] * u_imag + spec_h[1] * u_real
    mix_cols = (inverse_dft(prod_real, prod_imag, seq_len, tables) + gain[:, None] * gate_f).astype(
        jnp.bfloat16
    )
    return (mix_cols, (u_real, u_imag))


def grad_long(grad_cols_in, gate_cols, spec_u, spec_h, gain, seq_len, tables):
    grad_f = grad_cols_in.astype(jnp.float32)
    g_real, g_imag = forward_dft(grad_f, tables)
    back_real = spec_h[0] * g_real + spec_h[1] * g_imag
    back_imag = spec_h[0] * g_imag - spec_h[1] * g_real
    grad_cols = (
        inverse_dft(back_real, back_imag, seq_len, tables) + gain[:, None] * grad_f
    ).astype(jnp.bfloat16)
    corr_real = g_real * spec_u[0] + g_imag * spec_u[1]
    corr_imag = g_imag * spec_u[0] - g_real * spec_u[1]
    grad_filter = inverse_dft(corr_real, corr_imag, seq_len, tables)
    skip_sum = jnp.sum(grad_f * gate_cols.astype(jnp.float32), axis=1)
    return (grad_cols, grad_filter, skip_sum)


def body(projections, short_taps, residues, decay_rates, skip_gain, grad_mixed, out_weight):
    tokens = projections.shape[0]
    seq_len = tokens * lax.axis_size("ctx")
    norm_factor = math.sqrt(seq_len)
    tables = spectral_tables(2 * seq_len)
    earlier = from_behind(projections[tokens - SHORT + 1 :], "ctx", 1)
    ext_proj = jnp.concatenate([earlier, projections], axis=0)
    mixed_in = short_mix(ext_proj, short_taps, tokens)
    query_rows = mixed_in[:, 0]
    key_rows = mixed_in[:, 1]
    value_rows = mixed_in[:, 2]
    gated_rows = (key_rows * value_rows).astype(jnp.bfloat16)
    long_filter, filter_vjp = jax.vjp(partial(make_filter, seq_len=seq_len), residues, decay_rates)
    spec_h = forward_dft(long_filter, tables)
    out_rows = lax.all_gather(grad_mixed, "ch", axis=1, tiled=True)
    grad_out = lax.dot_general(
        out_rows,
        lax.all_gather(out_weight, "ctx", axis=1, tiled=True),
        (((1,), (1,)), ((), ())),
        preferred_element_type=jnp.float32,
    )
    grad_y = (grad_out * query_rows).astype(jnp.bfloat16)
    gate_cols, grad_cols_in = (
        lax.all_to_all(gated_rows.T, "ctx", split_axis=0, concat_axis=1, tiled=True),
        lax.all_to_all(grad_y.T, "ctx", split_axis=0, concat_axis=1, tiled=True),
    )
    mix_cols, spec_u = mix_long(gate_cols, spec_h, skip_gain, seq_len, tables)
    grad_cols, grad_filter, skip_sum = grad_long(
        grad_cols_in, gate_cols, spec_u, spec_h, skip_gain, seq_len, tables
    )
    returned = (
        lax.all_to_all(mix_cols, "ctx", split_axis=1, concat_axis=0, tiled=True),
        lax.all_to_all(grad_cols, "ctx", split_axis=1, concat_axis=0, tiled=True),
    )
    mix_rows = returned[0].T
    grad_gated = returned[1].T
    grad_res, grad_rate = filter_vjp(grad_filter)
    grad_residues = grad_res / norm_factor
    grad_log_rates = grad_rate * decay_rates / norm_factor
    grad_skip = skip_sum / norm_factor
    mixed_out = (query_rows * mix_rows).astype(jnp.bfloat16)
    grad_mix = jnp.stack(
        [grad_out * mix_rows, grad_gated * value_rows, grad_gated * key_rows], axis=1
    )
    later = from_behind(grad_mix[: SHORT - 1], "ctx", -1)
    ext_grad = jnp.concatenate([grad_mix, later], axis=0)
    running = jnp.zeros(grad_mix.shape, jnp.float32)
    short_terms = []
    for lag_index in range(SHORT):
        running = running + short_taps[lag_index] * ext_grad[lag_index : lag_index + tokens]
        start_row = SHORT - 1 - lag_index
        short_terms.append(jnp.sum(grad_mix * ext_proj[start_row : start_row + tokens], axis=0))
    grad_projections = running.astype(jnp.bfloat16)
    grad_short = lax.psum(jnp.stack(short_terms, axis=0), "ctx") / norm_factor
    partial_term = lax.dot_general(
        mixed_out, out_rows, (((0,), (0,)), ((), ())), preferred_element_type=jnp.float32
    )
    weight_sum = lax.psum_scatter(partial_term, "ctx", scatter_dimension=1, tiled=True)
    grad_weight = weight_sum / norm_factor
    return (grad_projections, grad_short, grad_skip, grad_residues, grad_log_rates, grad_weight)


def solution(mesh):
    return jax.shard_map(
        body,
        mesh=mesh,
        in_specs=(
            P(("groups", "ctx"), None, "ch"),
            P(None, None, "ch"),
            P(("ch", "ctx"), None),
            P(("ch", "ctx"), None),
            P(("ch", "ctx")),
            P(("groups", "ctx"), "ch"),
            P("ch", "ctx"),
        ),
        out_specs=(
            P(("groups", "ctx"), None, "ch"),
            P("groups", None, "ch"),
            P(("groups", "ch", "ctx")),
            P(("groups", "ch", "ctx"), None),
            P(("groups", "ch", "ctx"), None),
            P(("groups", "ch"), "ctx"),
        ),
        check_vma=False,
    )
```

profile of v0, /device:TPU:0, one launch (start us, length us, event | category | flops | bytes accessed | tf_op | source)
XLA Modules:
  0.0 378.1 jit_solution(4330585628768449797)
XLA Ops:
  8.7 4.9 %collective-permute-start = (bf16[2,3,1024]{2,0,1:T(2,128)(2,1)S(1)}, bf16[2,3,1024]{2,0,1:T(2,128)(2,1)S(1)}, u32[]{:S(2)}, u32[]{:S(2)}) collective-permute-start(bf16[2,3,1024]{2,0,1:T(2,128)(2,1)S(1)} %slice.52), channel_id=1, source_target_pairs={{0,4},{4,8},{8,12},{1,5},{5,9},{9,13},{2,6},{6,10},{10,14},{3,7},{... | collective-permute-start | bytes 36872 | tf_op jit(solution)/shard_map/ppermute | solution.py:14
  13.7 7.4 %all_gather.6 = bf16[128,2048]{1,0:T(8,128)(2,1)S(1)} all-gather(bf16[128,512]{1,0:T(8,128)(2,1)} %param.12), channel_id=1, replica_groups=mesh['groups'=2,'ctx'=4,'ch'=4] {'ch'}, dimensions={1}, use_global_device_ids=true | all-gather | bytes 655360 | tf_op jit(solution)/shard_map/all_gather | solution.py:126
  21.7 71.3 %all-gather.2.cloned.1.call-done = bf16[1024,2048]{1,0:T(8,128)(2,1)} async-done(((bf16[1024,512]{1,0:T(8,128)(2,1)}), bf16[1024,2048]{1,0:T(8,128)(2,1)}) %all-gather.2.cloned.1.call-update) | async-done | bytes 4194320 | tf_op jit(solution)/shard_map/all_gather | solution.py:129
  93.1 4.5 %multiply_convert_fusion.1 = (bf16[128,1024]{1,0:T(8,128)(2,1)S(1)}, bf16[128,1024]{1,0:T(8,128)(2,1)S(1)}, f32[128,1024]{1,0:T(8,128)}) fusion(f32[128,3,1024]{2,0,1:T(8,128)S(1)} %fusion.1, bf16[128,2048]{1,0:T(8,128)(2,1)S(1)} %all_gather.6, bf16[1024,2048]{1,0:T(8,128)(2,1)} %all-gather.2.cloned.1.call-done), kind=kOutput, calls=%fused_computation.133 | convolution fusion | flops 537395200 | bytes 7340032 | tf_op jit(solution)/shard_map/dot_general | solution.py:127
  98.4 3.4 all-to-all-start.2
  104.3 6.7 %all-to-all-done.2 = bf16[4,256,128]{1,2,0:T(8,128)(2,1)S(1)} async-done(((bf16[4,256,128]{1,2,0:T(8,128)(2,1)}), bf16[4,256,128]{1,2,0:T(8,128)(2,1)S(1)}, u32[]{:S(2)}, u32[]{:S(2)}) %all-to-all-start.2) | async-done | bytes 262176 | tf_op jit(solution)/shard_map/all_to_all | solution.py:136
  110.9 3.4 all-to-all-start
  137.8 3.1 multiply_add_fusion
  145.6 3.7 fusion.17
  149.3 3.7 fusion.8
  156.5 6.5 %multiply_reduce_fusion.2 = (f32[256,16]{1,0:T(8,128)}, f32[256,512]{1,0:T(8,128)}) fusion(f32[256,16]{1,0:T(8,128)} %copy.327, f32[256,512]{1,0:T(8,128)} %copy.328, f32[512]{0:T(512)S(1)} %iota_multiply_fusion.1, f32[256,16]{1,0:T(8,128)} %copy.203), kind=kLoop, calls=%fused_computation.2 | loop fusion | flops 14544896 | bytes 1099776 | tf_op jit(solution)/shard_map/transpose(jvp())/reduce_sum | solution.py:20
  186.9 3.7 fusion.31
  190.6 3.9 %fusion.11 = f32[256,32,32]{0,1,2:T(8,128)S(1)} fusion(f32[256,32,32]{0,2,1:T(8,128)S(1)} %fusion.31, f32[32,32]{0,1:T(8,128)S(1)} %copy.207, f32[32,32]{0,1:T(8,128)S(1)} %copy.205, f32[256,32,32]{0,2,1:T(8,128)S(1)} %fusion.98, f32[256,32,32]{0,2,1:T(8,128)S(1)} %fusion.122, f32[256,32,32]{0,2,1:T(8,128)S(1)} %fusion.96, f32[256,32,32]{0,2,1:T(8,128)S(1)} %fusion.120), kind=kOutput, calls=%fused_computation.32 | convolution fusion | flops 102250496 | bytes 6299648 | tf_op jit(solution)/shard_map/ak,ckb->cab/dot_general | solution.py:72
  195.1 3.7 fusion.24
  198.8 3.7 fusion.9
  204.3 11.1 %all_to_all.52 = bf16[256,4,128]{0,2,1:T(8,128)(2,1)S(1)} all-to-all(bf16[256,4,128]{0,2,1:T(8,128)(2,1)S(1)} %bitcast.240), channel_id=1, replica_groups=mesh['groups'=2,'ctx'=4,'ch'=4] {'ctx'}, dimensions={1} | all-to-all | bytes 524288 | tf_op jit(solution)/shard_map/all_to_all | solution.py:143
  215.5 4.5 %fusion.80 = f32[1024,2048]{1,0:T(8,128)} fusion(bf16[128,2048]{1,0:T(8,128)(2,1)S(1)} %all_gather.6, f32[1024,128]{0,1:T(8,128)S(1)} %bitcast.230, f32[128,3,1024]{2,0,1:T(8,128)S(1)} %fusion.1), kind=kOutput, calls=%fused_computation.146 | convolution fusion | flops 537133056 | bytes 9961472 | tf_op jit(solution)/shard_map/dot_general | solution.py:166
  220.1 3.6 all-to-all-start.3
  223.7 3.7 multiply_reduce_fusion
  228.3 8.6 %all-to-all-done.3 = bf16[256,4,128]{0,2,1:T(8,128)(2,1)S(1)} async-done(((bf16[256,4,128]{0,2,1:T(8,128)(2,1)}), bf16[256,4,128]{0,2,1:T(8,128)(2,1)S(1)}, u32[]{:S(2)}, u32[]{:S(2)}) %all-to-all-start.3) | async-done | bytes 262176 | tf_op jit(solution)/shard_map/all_to_all | solution.py:144
  240.2 7.0 %collective-permute-done.1 = f32[2,3,1024]{2,0,1:T(2,128)S(1)} collective-permute-done((f32[2,3,1024]{2,0,1:T(2,128)S(1)}, f32[2,3,1024]{2,0,1:T(2,128)S(1)}, u32[]{:S(2)}, u32[]{:S(2)}) %collective-permute-start.1) | collective-permute-done | bytes 24608 | tf_op jit(solution)/shard_map/ppermute | solution.py:14
  249.4 19.5 %psum.7 = f32[3,3,1024]{2,1,0:T(4,128)S(1)} all-reduce(f32[3,3,1024]{2,1,0:T(4,128)S(1)} %pad_maximum_fusion.3), channel_id=1, replica_groups=mesh['groups'=2,'ctx'=4,'ch'=4] {'ctx'}, use_global_device_ids=true, to_apply=%region_3.4 | all-reduce | flops 9216 | bytes 73728 | tf_op jit(solution)/shard_map/psum | solution.py:165
  269.6 98.2 %reduce-scatter.2.cloned.1.call-done = f32[1024,512]{1,0:T(8,128)} async-done(((f32[1024,2048]{1,0:T(8,128)}), f32[1024,512]{1,0:T(8,128)}) %reduce-scatter.2.cloned.1.call-update) | async-done | bytes 2097168 | tf_op jit(solution)/shard_map/reduce_scatter | solution.py:169
  367.8 3.2 broadcast_multiply_fusion
  (111 shorter events, 70.0 us)
Async XLA Ops:
  7.2 14.0 %copy-start.9 = (bf16[128,3,1024]{2,0,1:T(8,128)(2,1)S(1)}, bf16[128,3,1024]{2,0,1:T(8,128)(2,1)}, u32[]{:S(2)}) copy-start(bf16[128,3,1024]{2,0,1:T(8,128)(2,1)} %param.7) | copy-start | bytes 2359300
  7.2 13.9 %copy-start.15 = (f32[3,3,1024]{2,1,0:T(4,128)S(1)}, f32[3,3,1024]{2,1,0:T(4,128)}, u32[]{:S(2)}) copy-start(f32[3,3,1024]{2,1,0:T(4,128)} %param.8) | copy-start | bytes 110596
  7.2 85.9 %all-gather.2.cloned.1.call-start = ((), (), s32[]{:S(2)}) async-start(), calls=%async_computation.5 | async-start | bytes 5242880 | tf_op jit(solution)/shard_map/all_gather | solution.py:129
  8.7 12.4 %collective-permute-start = (bf16[2,3,1024]{2,0,1:T(2,128)(2,1)S(1)}, bf16[2,3,1024]{2,0,1:T(2,128)(2,1)S(1)}, u32[]{:S(2)}, u32[]{:S(2)}) collective-permute-start(bf16[2,3,1024]{2,0,1:T(2,128)(2,1)S(1)} %slice.52), channel_id=1, source_target_pairs={{0,4},{4,8},{8,12},{1,5},{5,9},{9,13},{2,6},{6,10},{10,14},{3,7},{... | collective-permute-start | bytes 36872 | tf_op jit(solution)/shard_map/ppermute | solution.py:14
  21.7 80.3 %copy-start.13 = (f32[256,16]{0,1:T(8,128)S(1)}, f32[256,16]{0,1:T(8,128)}, u32[]{:S(2)}) copy-start(f32[256,16]{0,1:T(8,128)} %param.10) | copy-start | bytes 49156
  21.7 80.3 %copy-start.14 = (f32[256,16]{0,1:T(8,128)S(1)}, f32[256,16]{0,1:T(8,128)}, u32[]{:S(2)}) copy-start(f32[256,16]{0,1:T(8,128)} %param.9) | copy-start | bytes 49156
  98.4 12.6 %all-to-all-start.2 = ((bf16[4,256,128]{1,2,0:T(8,128)(2,1)}), bf16[4,256,128]{1,2,0:T(8,128)(2,1)S(1)}, u32[]{:S(2)}, u32[]{:S(2)}) async-start(bf16[4,256,128]{1,2,0:T(8,128)(2,1)} %bitcast.222), calls=%async_computation.2 | async-start | bytes 524288 | tf_op jit(solution)/shard_map/all_to_all | solution.py:136
  110.9 10.3 %all-to-all-start = ((bf16[4,256,128]{1,2,0:T(8,128)(2,1)}), bf16[4,256,128]{1,2,0:T(8,128)(2,1)S(1)}, u32[]{:S(2)}, u32[]{:S(2)}) async-start(bf16[4,256,128]{1,2,0:T(8,128)(2,1)} %bitcast.223), calls=%async_computation | async-start | bytes 524288 | tf_op jit(solution)/shard_map/all_to_all | solution.py:135
  114.4 253.5 %reduce-scatter.2.cloned.1.call-start = ((), (), s32[]{:S(2)}) async-start(), calls=%async_computation.6 | async-start | bytes 10485760 | tf_op jit(solution)/shard_map/reduce_scatter | solution.py:169
  121.2 1.9 copy-start.4
  121.3 1.8 copy-start.6
  121.3 1.8 copy-start.7
  136.0 1.8 copy-start
  137.8 3.1 copy-start.2
  173.5 1.9 copy-start.1
  173.5 1.9 copy-start.3
  173.5 1.9 copy-start.8
  202.5 1.0 copy-start.5
  202.5 0.9 copy-start.16
  220.1 3.6 copy-start.11
  220.1 16.8 %all-to-all-start.3 = ((bf16[256,4,128]{0,2,1:T(8,128)(2,1)}), bf16[256,4,128]{0,2,1:T(8,128)(2,1)S(1)}, u32[]{:S(2)}, u32[]{:S(2)}) async-start(bf16[256,4,128]{0,2,1:T(8,128)(2,1)} %bitcast.54), calls=%async_computation.3 | async-start | bytes 524288 | tf_op jit(solution)/shard_map/all_to_all | solution.py:144
  223.6 3.8 %copy-start.12 = (f32[256,16]{1,0:T(8,128)S(1)}, f32[256,16]{1,0:T(8,128)}, u32[]{:S(2)}) copy-start(f32[256,16]{1,0:T(8,128)} %get-tuple-element.15) | copy-start | bytes 49156
  238.4 8.9 %collective-permute-start.1 = (f32[2,3,1024]{2,0,1:T(2,128)S(1)}, f32[2,3,1024]{2,0,1:T(2,128)S(1)}, u32[]{:S(2)}, u32[]{:S(2)}) collective-permute-start(f32[2,3,1024]{2,0,1:T(2,128)S(1)} %slice.72), channel_id=1, source_target_pairs={{4,0},{8,4},{12,8},{5,1},{9,5},{13,9},{6,2},{10,6},{14,10},{7,3},{... | collective-permute-start | bytes 73736 | tf_op jit(solution)/shard_map/ppermute | solution.py:14
  240.2 7.2 %copy-start.10 = (bf16[128,3,1024]{2,0,1:T(8,128)(2,1)S(1)}, bf16[128,3,1024]{2,0,1:T(8,128)(2,1)}, u32[]{:S(2)}) copy-start(bf16[128,3,1024]{2,0,1:T(8,128)(2,1)} %param.7) | copy-start | bytes 2359300
Sparse Core Ops, SparseCore 0:
  9.6 83.4 all-gather.1
  220.2 147.5 reduce-scatter.1
where the time goes:
time: 382 us; the launch traced here: 378 us
  waiting for transfers between devices  193 us (51%)
  matrix products  81.3 us (21%)
  blocking collectives  38.1 us (10%)
  other arithmetic  21.5 us (6%)
  starting transfers between devices  17.2 us (5%)
  between operations  15 us (4%)
  local copies, waits for them, and re-layouts  11.7 us (3%)
    reduce_scatter x1, waiting for transfers between devices, body(): lax.psum_scatter(partial_term, 'ctx', scatter_dimension=1, tiled=True)  98.2 us
    all_gather x1, waiting for transfers between devices, body(): lax.all_gather(out_weight, 'ctx', axis=1, tiled=True)  71.3 us
    psum x1, blocking collectives, body(): grad_short = lax.psum(jnp.stack(short_terms, axis=0), 'ctx') / norm_factor  19.5 us
    dot_general x3, matrix products, inverse_dft(): jnp.einsum('ak,ckb->cab', a_sin, turn_imag, precision=highest)  11.3 us
    all_to_all x1, blocking collectives, body(): lax.all_to_all(mix_cols, 'ctx', split_axis=1, concat_axis=0, tiled=True)  11.1 us
    dot_general x3, matrix products, inverse_dft(): jnp.einsum('ak,ckb->cab', a_cos, turn_real, precision=highest)  11.1 us
    all_to_all x1, waiting for transfers between devices, body(): lax.all_to_all(grad_cols, 'ctx', split_axis=1, concat_axis=0, tiled=True)  8.58 us
  transfers between devices with their start and end apart: 7, of which 6 were waited for; matrix products, arithmetic and copies ran while one was open for 5% of the time, Pallas kernels for 0%

commit v1 on v0

--- a/solution.py
+++ b/solution.py
@@ -6,6 +6,22 @@
 from jax.sharding import PartitionSpec as P
 
 SHORT = 3
+
+
+def collect(x, axis, dim):
+    ways, here, step = (lax.axis_size(axis), lax.axis_index(axis), x.shape[dim])
+    shape = [n * ways if d == dim else n for d, n in enumerate(x.shape)]
+    full = lax.dynamic_update_slice_in_dim(jnp.zeros(shape, x.dtype), x, here * step, axis=dim)
+    going_up = going_down = x
+    for far in range(1, ways // 2 + 1):
+        going_up = lax.ppermute(going_up, axis, [(d, (d + 1) % ways) for d in range(ways)])
+        full = lax.dynamic_update_slice_in_dim(full, going_up, (here - far) % ways * step, axis=dim)
+        if 2 * far < ways:
+            going_down = lax.ppermute(going_down, axis, [(d, (d - 1) % ways) for d in range(ways)])
+            full = lax.dynamic_update_slice_in_dim(
+                full, going_down, (here + far) % ways * step, axis=dim
+            )
+    return full
 
 
 def from_behind(x, axis, by):
@@ -126,7 +142,7 @@
     out_rows = lax.all_gather(grad_mixed, "ch", axis=1, tiled=True)
     grad_out = lax.dot_general(
         out_rows,
-        lax.all_gather(out_weight, "ctx", axis=1, tiled=True),
+        collect(out_weight, "ctx", 1),
         (((1,), (1,)), ((), ())),
         preferred_element_type=jnp.float32,
     )

time: 382 us -> 370 us (0.969)
  waiting for transfers between devices: 193 us -> 164 us
  local copies, waits for them, and re-layouts: 11.7 us -> 24.2 us
    all_gather x1 -> x0, waiting for transfers between devices: 71.3 us -> none  [body(): lax.all_gather(out_weight, 'ctx', axis=1, tiled=True)]
    ppermute x0 -> x3, waiting for transfers between devices: none -> 40.4 us  [the longest x2 40.4 us: collect(): lax.ppermute(going_up, axis, [(d, (d + 1) % ways) for d in range(ways)])]
    dynamic_update_slice x0 -> x4, local copies, waits for them, and re-layouts: none -> 8.06 us  [the longest x2 4.64 us: collect(): lax.dynamic_update_slice_in_dim(full, going_up, (here - far) % ways * ste...]
    ppermute x2, waiting for transfers between devices: 7.01 us -> 13.2 us  [from_behind(): return lax.ppermute(x, axis, pairs)]
    ppermute x0 -> x3, starting transfers between devices: none -> 5.17 us  [the longest x2 3.08 us: collect(): lax.ppermute(going_up, axis, [(d, (d + 1) % ways) for d in range(ways)])]
  transfers between devices with their start and end apart: 7 -> 9, of which waited for: 6 -> 8; matrix products, arithmetic and copies ran while one was open for 5% -> 8% of each run, Pallas kernels for 0% -> 0%
where the time goes in v1:
time: 370 us; the launch traced here: 365 us
  waiting for transfers between devices  164 us (44%)
  matrix products  81 us (22%)
  blocking collectives  40.4 us (11%)
  local copies, waits for them, and re-layouts  24.2 us (7%)
  other arithmetic  21.1 us (6%)
  starting transfers between devices  19.2 us (5%)
  between operations  15 us (4%)
    reduce_scatter x1, waiting for transfers between devices, body(): lax.psum_scatter(partial_term, 'ctx', scatter_dimension=1, tiled=True)  99.9 us
    ppermute x2, waiting for transfers between devices, collect(): lax.ppermute(going_up, axis, [(d, (d + 1) % ways) for d in range(ways)])  40.4 us
    psum x1, blocking collectives, body(): grad_short = lax.psum(jnp.stack(short_terms, axis=0), 'ctx') / norm_factor  21.5 us
    ppermute x2, waiting for transfers between devices, from_behind(): return lax.ppermute(x, axis, pairs)  13.2 us
    all_to_all x1, blocking collectives, body(): lax.all_to_all(mix_cols, 'ctx', split_axis=1, concat_axis=0, tiled=True)  11.3 us
    dot_general x3, matrix products, inverse_dft(): jnp.einsum('ak,ckb->cab', a_sin, turn_imag, precision=highest)  11.3 us
    dot_general x3, matrix products, inverse_dft(): jnp.einsum('ak,ckb->cab', a_cos, turn_real, precision=highest)  11 us
    all_gather x1, blocking collectives, body(): out_rows = lax.all_gather(grad_mixed, 'ch', axis=1, tiled=True)  7.61 us
  transfers between devices with their start and end apart: 9, of which 8 were waited for; matrix products, arithmetic and copies ran while one was open for 8% of the time, Pallas kernels for 0%

profile of v1, /device:TPU:0, one launch (start us, length us, event | category | flops | bytes accessed | tf_op | source)
XLA Modules:
  0.0 365.3 jit_solution(12339320621070315360)
XLA Ops:
  15.0 21.6 %collective-permute-done = bf16[1024,512]{1,0:T(8,128)(2,1)} collective-permute-done((bf16[1024,512]{1,0:T(8,128)(2,1)}, bf16[1024,512]{1,0:T(8,128)(2,1)}, u32[]{:S(2)}, u32[]{:S(2)}) %collective-permute-start) | collective-permute-done | bytes 1048608 | tf_op jit(solution)/shard_map/ppermute | solution.py:17
  36.6 7.6 %all_gather.3 = bf16[128,2048]{1,0:T(8,128)(2,1)S(1)} all-gather(bf16[128,512]{1,0:T(8,128)(2,1)} %param.12), channel_id=1, replica_groups=mesh['groups'=2,'ctx'=4,'ch'=4] {'ch'}, dimensions={1}, use_global_device_ids=true | all-gather | bytes 655360 | tf_op jit(solution)/shard_map/all_gather | solution.py:142
  48.0 8.8 %collective-permute-done.3 = bf16[2,3,1024]{2,0,1:T(2,128)(2,1)S(1)} collective-permute-done((bf16[2,3,1024]{2,0,1:T(2,128)(2,1)S(1)}, bf16[2,3,1024]{2,0,1:T(2,128)(2,1)S(1)}, u32[]{:S(2)}, u32[]{:S(2)}) %collective-permute-start.3) | collective-permute-done | bytes 12320 | tf_op jit(solution)/shard_map/ppermute | solution.py:30
  62.0 18.7 %collective-permute-done.2 = bf16[1024,512]{1,0:T(8,128)(2,1)} collective-permute-done((bf16[1024,512]{1,0:T(8,128)(2,1)}, bf16[1024,512]{1,0:T(8,128)(2,1)}, u32[]{:S(2)}, u32[]{:S(2)}) %collective-permute-start.2) | collective-permute-done | bytes 1048608 | tf_op jit(solution)/shard_map/ppermute | solution.py:17
  83.1 4.6 %multiply_convert_fusion.1 = (bf16[128,1024]{1,0:T(8,128)(2,1)S(1)}, bf16[128,1024]{1,0:T(8,128)(2,1)S(1)}, f32[128,1024]{1,0:T(8,128)}) fusion(f32[128,3,1024]{2,0,1:T(8,128)S(1)} %fusion.1, bf16[1024,2048]{1,0:T(8,128)(2,1)} %constant_dynamic-update-slice_fusion, bf16[128,2048]{1,0:T(8,128)(2,1)S(1)} %all_gather.3), kind=kOutput, calls=%fused_computation.134 | convolution fusion | flops 537395200 | bytes 7340032 | tf_op jit(solution)/shard_map/dot_general | solution.py:143
  88.3 3.4 all-to-all-start.2
  94.2 4.2 %all-to-all-done.2 = bf16[4,256,128]{1,2,0:T(8,128)(2,1)S(1)} async-done(((bf16[4,256,128]{1,2,0:T(8,128)(2,1)}), bf16[4,256,128]{1,2,0:T(8,128)(2,1)S(1)}, u32[]{:S(2)}, u32[]{:S(2)}) %all-to-all-start.2) | async-done | bytes 262176 | tf_op jit(solution)/shard_map/all_to_all | solution.py:152
  98.5 3.4 all-to-all-start
  132.9 3.7 %fusion.17 = f32[256,32,32]{0,2,1:T(8,128)S(1)} fusion(f32[32,32]{0,1:T(8,128)S(1)} %copy.207, f32[32,32]{0,1:T(8,128)S(1)} %copy.205, f32[256,32,32]{0,2,1:T(8,128)S(1)} %fusion.88, f32[256,32,32]{0,2,1:T(8,128)S(1)} %fusion.112, f32[256,32,32]{0,2,1:T(8,128)S(1)} %fusion.86, f32[256,32,32]{0,2,1:T(8,128)S(1)} %fusion.110), kind=kOutput, calls=%fused_computation.54 | convolution fusion | flops 101988352 | bytes 5251072 | tf_op jit(solution)/shard_map/ak,ckb->cab/dot_general | solution.py:88
  136.6 3.7 %fusion.8 = f32[256,32,32]{0,1,2:T(8,128)S(1)} fusion(f32[256,32,32]{0,2,1:T(8,128)S(1)} %fusion.17, f32[32,32]{0,1:T(8,128)S(1)} %copy.207, f32[32,32]{0,1:T(8,128)S(1)} %copy.205, f32[256,32,32]{0,2,1:T(8,128)S(1)} %fusion.88, f32[256,32,32]{0,2,1:T(8,128)S(1)} %fusion.112, f32[256,32,32]{0,2,1:T(8,128)S(1)} %fusion.86, f32[256,32,32]{0,2,1:T(8,128)S(1)} %fusion.110), kind=kOutput, calls=%fused_computation.23 | convolution fusion | flops 102250496 | bytes 6299648 | tf_op jit(solution)/shard_map/ak,ckb->cab/dot_general | solution.py:88
  143.8 6.5 %multiply_reduce_fusion.2 = (f32[256,16]{1,0:T(8,128)}, f32[256,512]{1,0:T(8,128)}) fusion(f32[256,16]{1,0:T(8,128)} %copy.327, f32[256,512]{1,0:T(8,128)} %copy.328, f32[512]{0:T(512)S(1)} %iota_multiply_fusion.1, f32[256,16]{1,0:T(8,128)} %copy.203), kind=kLoop, calls=%fused_computation.2 | loop fusion | flops 14544896 | bytes 1099776 | tf_op jit(solution)/shard_map/transpose(jvp())/reduce_sum | solution.py:36
  174.0 3.7 %fusion.31 = f32[256,32,32]{0,2,1:T(8,128)S(1)} fusion(f32[32,32]{0,1:T(8,128)S(1)} %copy.207, f32[32,32]{0,1:T(8,128)S(1)} %copy.205, f32[256,32,32]{0,2,1:T(8,128)S(1)} %fusion.98, f32[256,32,32]{0,2,1:T(8,128)S(1)} %fusion.122, f32[256,32,32]{0,2,1:T(8,128)S(1)} %fusion.96, f32[256,32,32]{0,2,1:T(8,128)S(1)} %fusion.120), kind=kOutput, calls=%fused_computation.74 | convolution fusion | flops 101988352 | bytes 5251072 | tf_op jit(solution)/shard_map/ak,ckb->cab/dot_general | solution.py:88
  177.7 3.9 %fusion.11 = f32[256,32,32]{0,1,2:T(8,128)S(1)} fusion(f32[256,32,32]{0,2,1:T(8,128)S(1)} %fusion.31, f32[32,32]{0,1:T(8,128)S(1)} %copy.207, f32[32,32]{0,1:T(8,128)S(1)} %copy.205, f32[256,32,32]{0,2,1:T(8,128)S(1)} %fusion.98, f32[256,32,32]{0,2,1:T(8,128)S(1)} %fusion.122, f32[256,32,32]{0,2,1:T(8,128)S(1)} %fusion.96, f32[256,32,32]{0,2,1:T(8,128)S(1)} %fusion.120), kind=kOutput, calls=%fused_computation.32 | convolution fusion | flops 102250496 | bytes 6299648 | tf_op jit(solution)/shard_map/ak,ckb->cab/dot_general | solution.py:88
  182.2 3.7 %fusion.24 = f32[256,32,32]{0,2,1:T(8,128)S(1)} fusion(f32[32,32]{0,1:T(8,128)S(1)} %copy.207, f32[32,32]{0,1:T(8,128)S(1)} %copy.205, f32[256,32,32]{0,2,1:T(8,128)S(1)} %fusion.92, f32[256,32,32]{0,2,1:T(8,128)S(1)} %fusion.116, f32[256,32,32]{0,2,1:T(8,128)S(1)} %fusion.90, f32[256,32,32]{0,2,1:T(8,128)S(1)} %fusion.114), kind=kOutput, calls=%fused_computation.63 | convolution fusion | flops 101988352 | bytes 5251072 | tf_op jit(solution)/shard_map/ak,ckb->cab/dot_general | solution.py:88
  185.9 3.7 %fusion.9 = f32[256,32,32]{0,1,2:T(8,128)S(1)} fusion(f32[256,32,32]{0,2,1:T(8,128)S(1)} %fusion.24, f32[32,32]{0,1:T(8,128)S(1)} %copy.207, f32[32,32]{0,1:T(8,128)S(1)} %copy.205, f32[256,32,32]{0,2,1:T(8,128)S(1)} %fusion.92, f32[256,32,32]{0,2,1:T(8,128)S(1)} %fusion.116, f32[256,32,32]{0,2,1:T(8,128)S(1)} %fusion.90, f32[256,32,32]{0,2,1:T(8,128)S(1)} %fusion.114), kind=kOutput, calls=%fused_computation.25 | convolution fusion | flops 102250496 | bytes 6299648 | tf_op jit(solution)/shard_map/ak,ckb->cab/dot_general | solution.py:88
  191.4 11.3 %all_to_all.52 = bf16[256,4,128]{0,2,1:T(8,128)(2,1)S(1)} all-to-all(bf16[256,4,128]{0,2,1:T(8,128)(2,1)S(1)} %bitcast.242), channel_id=1, replica_groups=mesh['groups'=2,'ctx'=4,'ch'=4] {'ctx'}, dimensions={1} | all-to-all | bytes 524288 | tf_op jit(solution)/shard_map/all_to_all | solution.py:159
  202.8 4.5 %fusion.80 = f32[1024,2048]{1,0:T(8,128)} fusion(bf16[128,2048]{1,0:T(8,128)(2,1)S(1)} %all_gather.3, f32[1024,128]{0,1:T(8,128)S(1)} %bitcast.232, f32[128,3,1024]{2,0,1:T(8,128)S(1)} %fusion.1), kind=kOutput, calls=%fused_computation.147 | convolution fusion | flops 537133056 | bytes 9961472 | tf_op jit(solution)/shard_map/dot_general | solution.py:182
  207.4 3.6 all-to-all-start.3
  210.9 4.2 %multiply_reduce_fusion = f32[256,16]{1,0:T(8,128)} fusion(f32[256,512]{1,0:T(8,128)S(1)} %copy-done.13, f32[512]{0:T(512)S(1)} %iota_multiply_fusion.1, f32[256,16]{1,0:T(8,128)} %copy.203), kind=kLoop, calls=%fused_computation | loop fusion | flops 6287360 | bytes 559104
  217.9 6.1 %all-to-all-done.3 = bf16[256,4,128]{0,2,1:T(8,128)(2,1)S(1)} async-done(((bf16[256,4,128]{0,2,1:T(8,128)(2,1)}), bf16[256,4,128]{0,2,1:T(8,128)(2,1)S(1)}, u32[]{:S(2)}, u32[]{:S(2)}) %all-to-all-start.3) | async-done | bytes 262176 | tf_op jit(solution)/shard_map/all_to_all | solution.py:160
  226.4 4.4 %collective-permute-done.4 = f32[2,3,1024]{2,0,1:T(2,128)S(1)} collective-permute-done((f32[2,3,1024]{2,0,1:T(2,128)S(1)}, f32[2,3,1024]{2,0,1:T(2,128)S(1)}, u32[]{:S(2)}, u32[]{:S(2)}) %collective-permute-start.4) | collective-permute-done | bytes 24608 | tf_op jit(solution)/shard_map/ppermute | solution.py:30
  233.0 21.5 %psum.7 = f32[3,3,1024]{2,1,0:T(4,128)S(1)} all-reduce(f32[3,3,1024]{2,1,0:T(4,128)S(1)} %pad_maximum_fusion.3), channel_id=1, replica_groups=mesh['groups'=2,'ctx'=4,'ch'=4] {'ctx'}, use_global_device_ids=true, to_apply=%region_3.4 | all-reduce | flops 9216 | bytes 73728 | tf_op jit(solution)/shard_map/psum | solution.py:181
  255.2 99.9 %reduce-scatter.2.cloned.1.call-done = f32[1024,512]{1,0:T(8,128)} async-done(((f32[1024,2048]{1,0:T(8,128)}), f32[1024,512]{1,0:T(8,128)}) %reduce-scatter.2.cloned.1.call-update) | async-done | bytes 2097168 | tf_op jit(solution)/shard_map/reduce_scatter | solution.py:185
  355.1 3.2 broadcast_multiply_fusion
  (121 shorter events, 90.5 us)
Async XLA Ops:
  7.2 29.5 %collective-permute-start = (bf16[1024,512]{1,0:T(8,128)(2,1)}, bf16[1024,512]{1,0:T(8,128)(2,1)}, u32[]{:S(2)}, u32[]{:S(2)}) collective-permute-start(bf16[1024,512]{1,0:T(8,128)(2,1)} %param.13), channel_id=1, source_target_pairs={{0,4},{4,8},{8,12},{12,0},{1,5},{5,9},{9,13},{13,1},{2,6},{6,10},{... | collective-permute-start | bytes 3145736 | tf_op jit(solution)/shard_map/ppermute | solution.py:17
  10.2 49.4 %collective-permute-start.1 = (bf16[1024,512]{1,0:T(8,128)(2,1)}, bf16[1024,512]{1,0:T(8,128)(2,1)}, u32[]{:S(2)}, u32[]{:S(2)}) collective-permute-start(bf16[1024,512]{1,0:T(8,128)(2,1)} %param.13), channel_id=1, source_target_pairs={{0,12},{4,0},{8,4},{12,8},{1,13},{5,1},{9,5},{13,9},{2,14},{6,2},{... | collective-permute-start | bytes 3145736 | tf_op jit(solution)/shard_map/ppermute | solution.py:20
  13.2 43.6 %collective-permute-start.3 = (bf16[2,3,1024]{2,0,1:T(2,128)(2,1)S(1)}, bf16[2,3,1024]{2,0,1:T(2,128)(2,1)S(1)}, u32[]{:S(2)}, u32[]{:S(2)}) collective-permute-start(bf16[2,3,1024]{2,0,1:T(2,128)(2,1)S(1)} %slice.52), channel_id=1, source_target_pairs={{0,4},{4,8},{8,12},{1,5},{5,9},{9,13},{2,6},{6,10},{10,14},{3,7},{... | collective-permute-start | bytes 36872 | tf_op jit(solution)/shard_map/ppermute | solution.py:30
  36.6 44.1 %collective-permute-start.2 = (bf16[1024,512]{1,0:T(8,128)(2,1)}, bf16[1024,512]{1,0:T(8,128)(2,1)}, u32[]{:S(2)}, u32[]{:S(2)}) collective-permute-start(bf16[1024,512]{1,0:T(8,128)(2,1)} %collective-permute-done), channel_id=1, source_target_pairs={{0,4},{4,8},{8,12},{12,0},{1,5},{5,9},{9,13},{13,1},{2,6},{6,10},{... | collective-permute-start | bytes 3145736 | tf_op jit(solution)/shard_map/ppermute | solution.py:17
  44.2 2.5 copy-start.12
  46.7 10.1 %copy-start.9 = (bf16[128,3,1024]{2,0,1:T(8,128)(2,1)S(1)}, bf16[128,3,1024]{2,0,1:T(8,128)(2,1)}, u32[]{:S(2)}) copy-start(bf16[128,3,1024]{2,0,1:T(8,128)(2,1)} %param.7) | copy-start | bytes 2359300
  83.0 8.9 %copy-start.14 = (f32[256,16]{0,1:T(8,128)S(1)}, f32[256,16]{0,1:T(8,128)}, u32[]{:S(2)}) copy-start(f32[256,16]{0,1:T(8,128)} %param.10) | copy-start | bytes 49156
  83.0 8.9 %copy-start.15 = (f32[256,16]{0,1:T(8,128)S(1)}, f32[256,16]{0,1:T(8,128)}, u32[]{:S(2)}) copy-start(f32[256,16]{0,1:T(8,128)} %param.9) | copy-start | bytes 49156
  88.3 10.2 %all-to-all-start.2 = ((bf16[4,256,128]{1,2,0:T(8,128)(2,1)}), bf16[4,256,128]{1,2,0:T(8,128)(2,1)S(1)}, u32[]{:S(2)}, u32[]{:S(2)}) async-start(bf16[4,256,128]{1,2,0:T(8,128)(2,1)} %bitcast.224), calls=%async_computation.2 | async-start | bytes 524288 | tf_op jit(solution)/shard_map/all_to_all | solution.py:152
  98.5 10.2 %all-to-all-start = ((bf16[4,256,128]{1,2,0:T(8,128)(2,1)}), bf16[4,256,128]{1,2,0:T(8,128)(2,1)S(1)}, u32[]{:S(2)}, u32[]{:S(2)}) async-start(bf16[4,256,128]{1,2,0:T(8,128)(2,1)} %bitcast.225), calls=%async_computation | async-start | bytes 524288 | tf_op jit(solution)/shard_map/all_to_all | solution.py:151
  101.9 253.2 %reduce-scatter.2.cloned.1.call-start = ((), (), s32[]{:S(2)}) async-start(), calls=%async_computation.5 | async-start | bytes 10485760 | tf_op jit(solution)/shard_map/reduce_scatter | solution.py:185
  108.7 1.9 copy-start.4
  108.7 1.8 copy-start.6
  108.8 1.8 copy-start.7
  123.4 1.8 copy-start
  125.1 3.1 copy-start.2
  160.7 1.8 copy-start.1
  160.7 1.8 copy-start.3
  160.7 1.8 copy-start.8
  207.3 3.6 copy-start.13
  207.4 16.6 %all-to-all-start.3 = ((bf16[256,4,128]{0,2,1:T(8,128)(2,1)}), bf16[256,4,128]{0,2,1:T(8,128)(2,1)S(1)}, u32[]{:S(2)}, u32[]{:S(2)}) async-start(bf16[256,4,128]{0,2,1:T(8,128)(2,1)} %bitcast.55), calls=%async_computation.3 | async-start | bytes 524288 | tf_op jit(solution)/shard_map/all_to_all | solution.py:160
  215.2 8.9 %copy-start.11 = (f32[128,1024]{1,0:T(8,128)S(1)}, f32[128,1024]{1,0:T(8,128)}, u32[]{:S(2)}) copy-start(f32[128,1024]{1,0:T(8,128)} %get-tuple-element.47) | copy-start | bytes 1572868
  224.6 6.2 %collective-permute-start.4 = (f32[2,3,1024]{2,0,1:T(2,128)S(1)}, f32[2,3,1024]{2,0,1:T(2,128)S(1)}, u32[]{:S(2)}, u32[]{:S(2)}) collective-permute-start(f32[2,3,1024]{2,0,1:T(2,128)S(1)} %slice.72), channel_id=1, source_target_pairs={{4,0},{8,4},{12,8},{5,1},{9,5},{13,9},{6,2},{10,6},{14,10},{7,3},{... | collective-permute-start | bytes 73736 | tf_op jit(solution)/shard_map/ppermute | solution.py:30
  226.4 4.6 %copy-start.10 = (bf16[128,3,1024]{2,0,1:T(8,128)(2,1)S(1)}, bf16[128,3,1024]{2,0,1:T(8,128)(2,1)}, u32[]{:S(2)}) copy-start(bf16[128,3,1024]{2,0,1:T(8,128)(2,1)} %param.7) | copy-start | bytes 2359300
  (3 other events, 3.0 us)
Sparse Core Ops, SparseCore 0:
  207.5 147.5 reduce-scatter.1
